TPU v7x, 32 devices: a whole 2x2x4 slice. The times are simulated.
32 devices in a mesh: dp: 4 (over y, x), context: 8 (over z, core).
Axes of the slice: x: 2, y: 2, z: 4, core: 2. Of those that a mesh axis runs over, the one named last changes fastest.
Arguments:
- projected: bfloat16 [4096, 6144], P(('dp', 'context')), may hold values from -6 to 6
- short_taps: float32 [3, 6144], replicated, may hold values from -4 to 4
- long_filter: float32 [2048, 1024], P('context'), may hold values from -1.5 to 1.5
- skip_gain: float32 [2048], P('context'), may hold values from -4 to 4
- out_proj: bfloat16 [2048, 2048], P('dp'), may hold values from -0.125 to 0.125
- cotangent: bfloat16 [4096, 2048], P(('dp', 'context')), may hold values from -25 to 25
Outputs:
- grad_inputs: bfloat16 [4096, 6144], P(('dp', 'context'))
- grad_taps: float32 [3, 6144], replicated
- grad_filter: float32 [2048, 1024], P('context', 'dp')
- grad_skip: float32 [2048], P('context')
- grad_proj: float32 [2048, 2048], P(('dp', 'context'))
All inputs are finite; a program needn't handle non-finite values.
Results may differ from a plain program's by a relative error of at most 0.012.
Values may be sent and summed in bfloat16 or wider, within the bound.
No kernel may reach another device: no remote copies, remote signals or barrier semaphores. Data moves between devices by JAX's collectives and lax.ppermute only.
A program may use at most 128 MiB of HBM per device.

v0:
```python
import math
import jax
import jax.numpy as jnp
from jax import lax
from jax.sharding import PartitionSpec as P

PRECISE = lax.Precision.HIGH


def passed_along(value, axis, steps):
    count = lax.axis_size(axis)
    initial, last = (max(0, -steps), min(count, count - steps))
    return lax.ppermute(value, axis, [(source, source + steps) for source in range(initial, last)])


def angle_table(first_count, second_count, period):
    first_idx = lax.broadcasted_iota(jnp.int32, (first_count, second_count), 0)
    second_idx = lax.broadcasted_iota(jnp.int32, (first_count, second_count), 1)
    phases = first_idx * second_idx % period
    angles = phases.astype(jnp.float32) * (-2.0 * math.pi / period)
    return (jnp.cos(angles), jnp.sin(angles))


def make_tables(seq_len):
    radix_size = min(128, seq_len)
    blocks = 2 * seq_len // radix_size
    half_blocks = blocks // 2
    outer_re, outer_im = angle_table(blocks, blocks, blocks)
    twist = angle_table(blocks, radix_size, blocks * radix_size)
    inner_re, inner_im = angle_table(radix_size, radix_size, radix_size)
    first_table = jnp.concatenate([outer_re[:, :half_blocks], outer_im[:, :half_blocks]], 0)
    inner_fwd = jnp.concatenate(
        [jnp.concatenate([inner_re, inner_im], 1), jnp.concatenate([-inner_im, inner_re], 1)], 0
    )
    inner_back = jnp.concatenate(
        [jnp.concatenate([inner_re, -inner_im], 1), jnp.concatenate([inner_im, inner_re], 1)], 0
    )
    last_table = jnp.concatenate([outer_re[:half_blocks, :], outer_im[:half_blocks, :]], 1)
    return (first_table, twist, inner_fwd, inner_back, last_table)


def forward_spectrum(signal, tables):
    first_table, (twist_re, twist_im), inner_fwd, inner_back, last_table = tables
    blocks = twist_re.shape[0]
    radix_size = twist_re.shape[1]
    shaped = signal.reshape(signal.shape[0], blocks // 2, radix_size)
    first = jnp.einsum("kn,cnm->ckm", first_table, shaped, precision=PRECISE)
    first_re = first[:, :blocks]
    first_im = first[:, blocks:]
    turned = jnp.concatenate(
        [first_re * twist_re - first_im * twist_im, first_re * twist_im + first_im * twist_re], 2
    )
    return jnp.einsum("ckn,nm->ckm", turned, inner_fwd, precision=PRECISE)


def spectral_product(left, right, conjugate_left):
    width = left.shape[2] // 2
    left_re, left_im = (left[:, :, :width], left[:, :, width:])
    right_re, right_im = (right[:, :, :width], right[:, :, width:])
    if conjugate_left:
        return jnp.concatenate(
            [left_re * right_re + left_im * right_im, left_re * right_im - left_im * right_re], 2
        )
    return jnp.concatenate(
        [left_re * right_re - left_im * right_im, left_re * right_im + left_im * right_re], 2
    )


def inverse_real(spectrum, tables):
    first_table, (twist_re, twist_im), inner_fwd, inner_back, last_table = tables
    blocks = twist_re.shape[0]
    radix_size = twist_re.shape[1]
    undo = jnp.einsum("ckn,nm->ckm", spectrum, inner_back, precision=PRECISE)
    undo_re = undo[:, :, :radix_size]
    undo_im = undo[:, :, radix_size:]
    back = jnp.concatenate(
        [undo_re * twist_re + undo_im * twist_im, undo_im * twist_re - undo_re * twist_im], 1
    )
    result = jnp.einsum("nk,ckm->cnm", last_table, back, precision=PRECISE)
    return result.reshape(spectrum.shape[0], blocks // 2 * radix_size) / (blocks * radix_size)


def body(projected, short_taps, long_filter, skip_gain, out_proj, cotangent):
    tok_rows = projected.shape[0]
    chan_all = projected.shape[1] // 3
    prev_rows = passed_along(projected[tok_rows - 2 :], "context", 1)
    extended = jnp.concatenate([prev_rows, projected], 0).astype(jnp.float32)
    current = extended[2:]
    once_back = extended[1 : tok_rows + 1]
    twice_back = extended[:tok_rows]
    mixed = short_taps[0] * current + short_taps[1] * once_back + short_taps[2] * twice_back
    query = mixed[:, :chan_all].astype(jnp.bfloat16)
    keyed = mixed[:, chan_all : 2 * chan_all].astype(jnp.bfloat16)
    valued = mixed[:, 2 * chan_all :].astype(jnp.bfloat16)
    product = (keyed.astype(jnp.float32) * valued.astype(jnp.float32)).astype(jnp.bfloat16)
    product_chan = lax.all_to_all(product.T, "context", split_axis=0, concat_axis=1, tiled=True)
    seq_len = product_chan.shape[1]
    tables = make_tables(seq_len)
    prod_f = product_chan.astype(jnp.float32)
    filter_spec = forward_spectrum(long_filter, tables)
    prod_spec = forward_spectrum(prod_f, tables)
    long_chan = (
        inverse_real(spectral_product(filter_spec, prod_spec, False), tables)
        + skip_gain[:, None] * prod_f
    )
    long_tok = lax.all_to_all(
        long_chan.astype(jnp.bfloat16), "context", split_axis=1, concat_axis=0, tiled=True
    ).T
    gate = (query.astype(jnp.float32) * long_tok.astype(jnp.float32)).astype(jnp.bfloat16)
    grad_gate = lax.dot_general(
        cotangent,
        lax.all_gather(out_proj, "dp", axis=0, tiled=True),
        (((1,), (1,)), ((), ())),
        preferred_element_type=jnp.float32,
    ).astype(jnp.bfloat16)
    grad_rows = lax.psum_scatter(
        lax.dot_general(
            gate, cotangent, (((0,), (0,)), ((), ())), preferred_element_type=jnp.float32
        ),
        ("dp", "context"),
        scatter_dimension=0,
        tiled=True,
    )
    grad_query = grad_gate.astype(jnp.float32) * long_tok.astype(jnp.float32)
    grad_long = (grad_gate.astype(jnp.float32) * query.astype(jnp.float32)).astype(jnp.bfloat16)
    grad_chan = lax.all_to_all(
        grad_long.T, "context", split_axis=0, concat_axis=1, tiled=True
    ).astype(jnp.float32)
    grad_spec = forward_spectrum(grad_chan, tables)
    back_chan = (
        inverse_real(spectral_product(filter_spec, grad_spec, True), tables)
        + skip_gain[:, None] * grad_chan
    )
    filter_local = inverse_real(spectral_product(prod_spec, grad_spec, True), tables)
    grad_product = lax.all_to_all(
        back_chan.astype(jnp.bfloat16), "context", split_axis=1, concat_axis=0, tiled=True
    ).T
    scale_factor = 1.0 / math.sqrt(seq_len * lax.axis_size("dp"))
    grad_filter = (
        lax.psum_scatter(filter_local, "dp", scatter_dimension=1, tiled=True) * scale_factor
    )
    grad_skip = lax.psum(jnp.sum(grad_chan * prod_f, axis=1), "dp") * scale_factor
    grad_key = grad_product.astype(jnp.float32) * valued.astype(jnp.float32)
    grad_value = grad_product.astype(jnp.float32) * keyed.astype(jnp.float32)
    grad_mixed = jnp.concatenate([grad_query, grad_key, grad_value], 1)
    next_rows = passed_along(grad_mixed[:2].astype(jnp.bfloat16), "context", -1).astype(jnp.float32)
    grad_ext = jnp.concatenate([grad_mixed, next_rows], 0)
    grad_inputs = (
        short_taps[0] * grad_ext[:tok_rows]
        + short_taps[1] * grad_ext[1 : tok_rows + 1]
        + short_taps[2] * grad_ext[2:]
    ).astype(jnp.bfloat16)
    taps_terms = jnp.stack(
        [
            jnp.sum(grad_mixed * current, 0),
            jnp.sum(grad_mixed * once_back, 0),
            jnp.sum(grad_mixed * twice_back, 0),
        ]
    )
    grad_taps = lax.psum(taps_terms, ("dp", "context")) * scale_factor
    return (grad_inputs, grad_taps, grad_filter, grad_skip, grad_rows * scale_factor)


def solution(mesh):
    placed = (
        P(("dp", "context"), None),
        P(),
        P("context", None),
        P("context"),
        P("dp", None),
        P(("dp", "context"), None),
    )
    return jax.shard_map(
        body,
        mesh=mesh,
        in_specs=placed,
        out_specs=(
            P(("dp", "context"), None),
            P(),
            P("context", "dp"),
            P("context"),
            P(("dp", "context"), None),
        ),
        check_vma=False,
    )
```

profile of v0, /device:TPU:0, one launch (start us, length us, event | category | flops | bytes accessed | tf_op | source)
XLA Modules:
  0.0 625.5 jit_solution(3541810269681701199)
XLA Ops:
  15.6 84.6 %all-gather.2.cloned.1.call-done = bf16[2048,2048]{1,0:T(8,128)(2,1)} async-done(((bf16[512,2048]{1,0:T(8,128)(2,1)}), bf16[2048,2048]{1,0:T(8,128)(2,1)}) %all-gather.2.cloned.1.call-update) | async-done | bytes 8388624 | tf_op jit(solution)/shard_map/all_gather | solution.py:112
  100.2 6.2 fusion.21
  108.6 4.6 all-to-all-start.2
  115.5 3.9 convolution_bitcast_fusion.2
  119.5 9.1 %all-to-all-done.2 = bf16[8,256,128]{2,1,0:T(8,128)(2,1)S(1)} async-done(((bf16[8,256,128]{2,1,0:T(8,128)(2,1)}), bf16[8,256,128]{2,1,0:T(8,128)(2,1)S(1)}, u32[]{:S(2)}, u32[]{:S(2)}) %all-to-all-start.2) | async-done | bytes 524320 | tf_op jit(solution)/shard_map/all_to_all | solution.py:126
  132.6 4.2 fusion.16
  136.8 4.2 fusion.12
  145.5 5.5 copy.61
  151.0 4.0 fusion.68
  159.0 17.8 %all_to_all.52 = bf16[256,8,128]{2,0,1:T(8,128)(2,1)S(1)} all-to-all(bf16[256,8,128]{2,0,1:T(8,128)(2,1)S(1)} %copy.52), channel_id=1, replica_groups=mesh['dp'=4,'context'=8] {'context'}, dimensions={1} | all-to-all | bytes 1048576 | tf_op jit(solution)/shard_map/all_to_all | solution.py:135
  181.2 17.8 %all_to_all.53 = bf16[8,256,128]{2,1,0:T(8,128)(2,1)S(1)} all-to-all(bf16[8,256,128]{2,1,0:T(8,128)(2,1)S(1)} %bitcast.96), channel_id=1, replica_groups=mesh['dp'=4,'context'=8] {'context'}, dimensions={0} | all-to-all | bytes 1048576 | tf_op jit(solution)/shard_map/all_to_all | solution.py:96
  202.0 4.1 fusion.14
  206.1 4.4 multiply_add_fusion.1
  210.5 4.6 pad_maximum_fusion.5
  215.1 5.5 copy.64
  220.6 6.1 fusion.66
  229.0 5.6 copy.58
  234.7 4.3 fusion.70
  245.1 17.8 %all_to_all.54 = bf16[256,8,128]{2,0,1:T(8,128)(2,1)S(1)} all-to-all(bf16[256,8,128]{2,0,1:T(8,128)(2,1)S(1)} %copy.43), channel_id=1, replica_groups=mesh['dp'=4,'context'=8] {'context'}, dimensions={1} | all-to-all | bytes 1048576 | tf_op jit(solution)/shard_map/all_to_all | solution.py:106
  282.0 9.1 %fusion.53 = f32[2048,2048]{1,0:T(8,128)} fusion(bf16[128,2048]{1,0:T(8,128)(2,1)S(1)} %copy-done, f32[2048,128]{0,1:T(8,128)S(1)} %copy-done.10, bf16[128,6144]{1,0:T(8,128)(2,1)} %copy-done.12), kind=kOutput, calls=%fused_computation.82 | convolution fusion | flops 1074528256 | bytes 18874368 | tf_op jit(solution)/shard_map/dot_general | solution.py:117
  293.5 8.9 %psum.15 = f32[256]{0:T(256)S(1)} all-reduce(f32[256]{0:T(256)S(1)} %fusion.52), channel_id=1, replica_groups=mesh['dp'=4,'context'=8] {'dp'}, use_global_device_ids=true, to_apply=%region_6.7 | all-reduce | flops 256 | bytes 2048 | tf_op jit(solution)/shard_map/psum | solution.py:142
  303.0 93.5 %all-reduce.2.cloned.1.call-done = f32[3,6144]{1,0:T(4,128)} async-done(((f32[3,6144]{1,0:T(4,128)}), f32[3,6144]{1,0:T(4,128)}) %all-reduce.2.cloned.1.call-update) | async-done | bytes 73744 | tf_op jit(solution)/shard_map/psum | solution.py:160
  398.0 29.9 %reduce-scatter.3.cloned.1.call-done = f32[256,256]{1,0:T(8,128)} async-done(((f32[256,1024]{1,0:T(8,128)}), f32[256,256]{1,0:T(8,128)}) %reduce-scatter.3.cloned.1.call-update) | async-done | bytes 262160 | tf_op jit(solution)/shard_map/reduce_scatter | solution.py:140
  429.6 187.3 %reduce-scatter.5.cloned.1.call-done = f32[64,2048]{1,0:T(8,128)} async-done(((f32[2048,2048]{1,0:T(8,128)}), f32[64,2048]{1,0:T(8,128)}) %reduce-scatter.5.cloned.1.call-update) | async-done | bytes 524304 | tf_op jit(solution)/shard_map/reduce_scatter | solution.py:116
  (108 shorter events, 67.9 us)
Async XLA Ops:
  7.2 93.1 %copy-start = (bf16[128,2048]{1,0:T(8,128)(2,1)S(1)}, bf16[128,2048]{1,0:T(8,128)(2,1)}, u32[]{:S(2)}) copy-start(bf16[128,2048]{1,0:T(8,128)(2,1)} %param.11) | copy-start | bytes 1572868
  7.2 5.3 copy-start.20
  7.2 93.0 %all-gather.2.cloned.1.call-start = ((), (), s32[]{:S(2)}) async-start(), calls=%async_computation.6 | async-start | bytes 10485760 | tf_op jit(solution)/shard_map/all_gather | solution.py:112
  8.8 3.6 collective-permute-start
  12.9 1.7 copy-start.1
  15.6 90.9 %copy-start.12 = (bf16[128,6144]{1,0:T(8,128)(2,1)}, bf16[128,6144]{1,0:T(8,128)(2,1)S(1)}, u32[]{:S(2)}) copy-start(bf16[128,6144]{1,0:T(8,128)(2,1)S(1)} %add_convert_fusion) | copy-start | bytes 4718596
  108.6 20.0 %all-to-all-start.2 = ((bf16[8,256,128]{2,1,0:T(8,128)(2,1)}), bf16[8,256,128]{2,1,0:T(8,128)(2,1)S(1)}, u32[]{:S(2)}, u32[]{:S(2)}) async-start(bf16[8,256,128]{2,1,0:T(8,128)(2,1)} %bitcast.17), calls=%async_computation.2 | async-start | bytes 1048576 | tf_op jit(solution)/shard_map/all_to_all | solution.py:126
  113.2 283.3 %all-reduce.2.cloned.1.call-start = ((), (), s32[]{:S(2)}) async-start(), calls=%async_computation.7 | async-start | bytes 196608 | tf_op jit(solution)/shard_map/psum | solution.py:160
  128.6 26.9 %copy-start.13 = (bf16[8,256,128]{2,1,0:T(8,128)(2,1)}, bf16[8,256,128]{2,1,0:T(8,128)(2,1)S(1)}, u32[]{:S(2)}) copy-start(bf16[8,256,128]{2,1,0:T(8,128)(2,1)S(1)} %all-to-all-done.2) | copy-start | bytes 1572868
  128.6 2.4 copy-start.7
  136.8 4.2 copy-start.3
  141.0 1.9 copy-start.5
  201.9 4.1 copy-start.4
  202.0 4.1 copy-start.6
  220.6 6.1 copy-start.18
  220.6 6.1 copy-start.19
  234.7 4.3 copy-start.8
  239.0 2.8 copy-start.16
  262.9 5.3 copy-start.9
  268.4 3.1 collective-permute-start.1
  271.5 1.9 copy-start.2
  277.2 150.8 %reduce-scatter.3.cloned.1.call-start = ((), (), s32[]{:S(2)}) async-start(), calls=%async_computation.8 | async-start | bytes 1310720 | tf_op jit(solution)/shard_map/reduce_scatter | solution.py:140
  277.3 4.8 copy-start.10
  282.0 334.9 %reduce-scatter.5.cloned.1.call-start = ((), (), s32[]{:S(2)}) async-start(), calls=%async_computation.9 | async-start | bytes 17301504 | tf_op jit(solution)/shard_map/reduce_scatter | solution.py:116
  (5 other events, 4.7 us)
Sparse Core Ops, SparseCore 0:
  9.9 90.2 all-gather.1
  277.3 119.1 all-reduce.1
  399.4 28.5 reduce-scatter.2
  430.2 186.6 reduce-scatter.4
where the time goes:
time: 631 us; the launch traced here: 626 us
  waiting for transfers between devices  407 us (65%)
  blocking collectives  62.2 us (10%)
  matrix products  58.9 us (9%)
  other arithmetic  39.3 us (6%)
  local copies, waits for them, and re-layouts  35.3 us (6%)
  between operations  14.5 us (2%)
  starting transfers between devices  8.42 us (1%)
    reduce_scatter x1, waiting for transfers between devices, body(): lax.psum_scatter(lax.dot_general(gate, cotangent, (((0,), (0,)), ((), ())...  187 us
    psum x1, waiting for transfers between devices, body(): grad_taps = lax.psum(taps_terms, ('dp', 'context')) * scale_factor  93.5 us
    all_gather x1, waiting for transfers between devices, body(): lax.all_gather(out_proj, 'dp', axis=0, tiled=True)  84.6 us
    reduce_scatter x1, waiting for transfers between devices, body(): lax.psum_scatter(filter_local, 'dp', scatter_dimension=1, tiled=True)  29.9 us
    all_to_all x1, blocking collectives, body(): lax.all_to_all(back_chan.astype(jnp.bfloat16), 'context', split_axis=1, c...  17.8 us
    all_to_all x1, blocking collectives, body(): lax.all_to_all(product.T, 'context', split_axis=0, concat_axis=1, tiled=T...  17.8 us
    all_to_all x1, blocking collectives, body(): lax.all_to_all(long_chan.astype(jnp.bfloat16), 'context', split_axis=1, c...  17.8 us
    dot_general x3, matrix products, inverse_real(): undo = jnp.einsum('ckn,nm->ckm', spectrum, inner_back, precision=PRECISE)  14.4 us
  transfers between devices with their start and end apart: 7, of which 6 were waited for; matrix products, arithmetic and copies ran while one was open for 5% of the time, Pallas kernels for 0%

commit v1 on v0

--- a/solution.py
+++ b/solution.py
@@ -93,7 +93,20 @@
     keyed = mixed[:, chan_all : 2 * chan_all].astype(jnp.bfloat16)
     valued = mixed[:, 2 * chan_all :].astype(jnp.bfloat16)
     product = (keyed.astype(jnp.float32) * valued.astype(jnp.float32)).astype(jnp.bfloat16)
-    product_chan = lax.all_to_all(product.T, "context", split_axis=0, concat_axis=1, tiled=True)
+    ways, here = (lax.axis_size("context"), lax.axis_index("context"))
+    width_2 = product.T.shape[0] // ways
+    dims = list(product.T.shape)
+    dims[0] = width_2
+    height = dims[1]
+    dims[1] = height * ways
+    product_chan = jnp.zeros(dims, product.T.dtype)
+    for mask in range(ways):
+        part = lax.dynamic_slice_in_dim(product.T, (here ^ mask) * width_2, width_2, axis=0)
+        if mask:
+            part = lax.ppermute(part, "context", [(d, d ^ mask) for d in range(ways)])
+        product_chan = lax.dynamic_update_slice_in_dim(
+            product_chan, part, (here ^ mask) * height, axis=1
+        )
     seq_len = product_chan.shape[1]
     tables = make_tables(seq_len)
     prod_f = product_chan.astype(jnp.float32)

time: 631 us -> 630 us (level)
  blocking collectives: 62.2 us -> 28.9 us
  waiting for transfers between devices: 407 us -> 428 us
  starting transfers between devices: 8.42 us -> 20.4 us
    all_to_all x2 -> x0, blocking collectives: 35.5 us -> none  [the longest x1 17.8 us: body(): lax.all_to_all(back_chan.astype(jnp.bfloat16), 'context', split_axis=1, c...]
    all_to_all x0 -> x1, waiting for transfers between devices: none -> 13.4 us  [body(): lax.all_to_all(back_chan.astype(jnp.bfloat16), 'context', split_axis=1, c...]
    ppermute x0 -> x7, starting transfers between devices: none -> 8.26 us  [body(): part = lax.ppermute(part, 'context', [(d, d ^ mask) for d in range(ways)])]
  transfers between devices with their start and end apart: 7 -> 15, of which waited for: 6 -> 9; matrix products, arithmetic and copies ran while one was open for 5% -> 5% of each run, Pallas kernels for 0% -> 0%
where the time goes in v1:
time: 630 us; the launch traced here: 624 us
  waiting for transfers between devices  428 us (68%)
  matrix products  57.9 us (9%)
  other arithmetic  37.9 us (6%)
  local copies, waits for them, and re-layouts  36.4 us (6%)
  blocking collectives  28.9 us (5%)
  starting transfers between devices  20.4 us (3%)
  between operations  14.7 us (2%)
    reduce_scatter x1, waiting for transfers between devices, body(): lax.psum_scatter(lax.dot_general(gate, cotangent, (((0,), (0,)), ((), ())...  187 us
    psum x1, waiting for transfers between devices, body(): grad_taps = lax.psum(taps_terms, ('dp', 'context')) * scale_factor  95.7 us
    all_gather x1, waiting for transfers between devices, body(): lax.all_gather(out_proj, 'dp', axis=0, tiled=True)  84.6 us
    reduce_scatter x1, waiting for transfers between devices, body(): lax.psum_scatter(filter_local, 'dp', scatter_dimension=1, tiled=True)  29.9 us
    all_to_all x1, blocking collectives, body(): lax.all_to_all(long_chan.astype(jnp.bfloat16), 'context', split_axis=1, c...  19.9 us
    dot_general x3, matrix products, inverse_real(): undo = jnp.einsum('ckn,nm->ckm', spectrum, inner_back, precision=PRECISE)  14.4 us
    all_to_all x1, waiting for transfers between devices, body(): lax.all_to_all(back_chan.astype(jnp.bfloat16), 'context', split_axis=1, c...  13.4 us
  transfers between devices with their start and end apart: 15, of which 9 were waited for; matrix products, arithmetic and copies ran while one was open for 5% of the time, Pallas kernels for 0%

profile of v1, /device:TPU:0, one launch (start us, length us, event | category | flops | bytes accessed | tf_op | source)
XLA Modules:
  0.0 624.0 jit_solution(17891902546666349391)
XLA Ops:
  15.6 84.6 %all-gather.2.cloned.1.call-done = bf16[2048,2048]{1,0:T(8,128)(2,1)} async-done(((bf16[512,2048]{1,0:T(8,128)(2,1)}), bf16[2048,2048]{1,0:T(8,128)(2,1)}) %all-gather.2.cloned.1.call-update) | async-done | bytes 8388624 | tf_op jit(solution)/shard_map/all_gather | solution.py:125
  100.2 6.3 %fusion.21 = f32[128,2048]{1,0:T(8,128)S(1)} fusion(bf16[128,2048]{1,0:T(8,128)(2,1)S(1)} %copy-done, bf16[2048,2048]{1,0:T(8,128)(2,1)} %all-gather.2.cloned.1.call-done), kind=kOutput, calls=%fused_computation.36 | convolution fusion | flops 1074266112 | bytes 9961472 | tf_op jit(solution)/shard_map/dot_general | solution.py:123
  108.6 4.6 all-to-all-start.1
  115.5 4.0 convolution_bitcast_fusion.2
  119.6 9.0 %all-to-all-done.1 = bf16[8,256,128]{2,1,0:T(8,128)(2,1)S(1)} async-done(((bf16[8,256,128]{2,1,0:T(8,128)(2,1)}), bf16[8,256,128]{2,1,0:T(8,128)(2,1)S(1)}, u32[]{:S(2)}, u32[]{:S(2)}) %all-to-all-start.1) | async-done | bytes 524320 | tf_op jit(solution)/shard_map/all_to_all | solution.py:139
  132.4 4.2 fusion.16
  136.6 4.2 fusion.12
  145.4 5.4 copy.88
  150.8 4.0 fusion.61
  165.0 13.4 %all-to-all-done.2 = bf16[256,8,128]{2,0,1:T(8,128)(2,1)S(1)} async-done(((bf16[256,8,128]{2,0,1:T(8,128)(2,1)}), bf16[256,8,128]{2,0,1:T(8,128)(2,1)S(1)}, u32[]{:S(2)}, u32[]{:S(2)}) %all-to-all-start.2) | async-done | bytes 524320 | tf_op jit(solution)/shard_map/all_to_all | solution.py:148
  191.1 4.5 collective-permute-done.4
  199.0 4.1 fusion.14
  203.1 4.5 multiply_add_fusion.1
  207.6 4.6 pad_maximum_fusion.2
  212.1 5.7 copy.85
  217.9 6.1 fusion.63
  226.3 5.5 copy.91
  231.8 4.3 fusion.59
  245.4 19.9 %all_to_all.39 = bf16[256,8,128]{0,2,1:T(8,128)(2,1)S(1)} all-to-all(bf16[256,8,128]{0,2,1:T(8,128)(2,1)S(1)} %bitcast.111), channel_id=1, replica_groups=mesh['dp'=4,'context'=8] {'context'}, dimensions={1} | all-to-all | bytes 1048576 | tf_op jit(solution)/shard_map/all_to_all | solution.py:119
  280.6 9.2 %fusion.49 = f32[2048,2048]{1,0:T(8,128)} fusion(bf16[128,2048]{1,0:T(8,128)(2,1)S(1)} %copy-done, f32[2048,128]{0,1:T(8,128)S(1)} %bitcast.105, bf16[128,6144]{1,0:T(8,128)(2,1)} %copy-done.12), kind=kOutput, calls=%fused_computation.82 | convolution fusion | flops 1074528256 | bytes 18874368 | tf_op jit(solution)/shard_map/dot_general | solution.py:130
  289.7 8.9 %psum.15 = f32[256]{0:T(256)S(1)} all-reduce(f32[256]{0:T(256)S(1)} %get-tuple-element.32), channel_id=1, replica_groups=mesh['dp'=4,'context'=8] {'dp'}, use_global_device_ids=true, to_apply=%region_6.7 | all-reduce | flops 256 | bytes 2048 | tf_op jit(solution)/shard_map/psum | solution.py:155
  299.3 95.7 %all-reduce.2.cloned.1.call-done = f32[3,6144]{1,0:T(4,128)} async-done(((f32[3,6144]{1,0:T(4,128)}), f32[3,6144]{1,0:T(4,128)}) %all-reduce.2.cloned.1.call-update) | async-done | bytes 73744 | tf_op jit(solution)/shard_map/psum | solution.py:173
  396.5 29.9 %reduce-scatter.3.cloned.1.call-done = f32[256,256]{1,0:T(8,128)} async-done(((f32[256,1024]{1,0:T(8,128)}), f32[256,256]{1,0:T(8,128)}) %reduce-scatter.3.cloned.1.call-update) | async-done | bytes 262160 | tf_op jit(solution)/shard_map/reduce_scatter | solution.py:153
  428.1 187.3 %reduce-scatter.5.cloned.1.call-done = f32[64,2048]{1,0:T(8,128)} async-done(((f32[2048,2048]{1,0:T(8,128)}), f32[64,2048]{1,0:T(8,128)}) %reduce-scatter.5.cloned.1.call-update) | async-done | bytes 524304 | tf_op jit(solution)/shard_map/reduce_scatter | solution.py:129
  (128 shorter events, 79.4 us)
Async XLA Ops:
  7.2 93.1 %copy-start = (bf16[128,2048]{1,0:T(8,128)(2,1)S(1)}, bf16[128,2048]{1,0:T(8,128)(2,1)}, u32[]{:S(2)}) copy-start(bf16[128,2048]{1,0:T(8,128)(2,1)} %param.11) | copy-start | bytes 1572868
  7.2 5.2 copy-start.17
  7.2 93.0 %all-gather.2.cloned.1.call-start = ((), (), s32[]{:S(2)}) async-start(), calls=%async_computation.5 | async-start | bytes 10485760 | tf_op jit(solution)/shard_map/all_gather | solution.py:125
  8.8 3.6 collective-permute-start
  15.6 90.9 %copy-start.12 = (bf16[128,6144]{1,0:T(8,128)(2,1)}, bf16[128,6144]{1,0:T(8,128)(2,1)S(1)}, u32[]{:S(2)}) copy-start(bf16[128,6144]{1,0:T(8,128)(2,1)S(1)} %add_convert_fusion) | copy-start | bytes 4718596
  108.6 20.0 %all-to-all-start.1 = ((bf16[8,256,128]{2,1,0:T(8,128)(2,1)}), bf16[8,256,128]{2,1,0:T(8,128)(2,1)S(1)}, u32[]{:S(2)}, u32[]{:S(2)}) async-start(bf16[8,256,128]{2,1,0:T(8,128)(2,1)} %bitcast.24), calls=%async_computation.1 | async-start | bytes 1048576 | tf_op jit(solution)/shard_map/all_to_all | solution.py:139
  136.6 4.2 copy-start.3
  159.6 18.8 %all-to-all-start.2 = ((bf16[256,8,128]{2,0,1:T(8,128)(2,1)}), bf16[256,8,128]{2,0,1:T(8,128)(2,1)S(1)}, u32[]{:S(2)}, u32[]{:S(2)}) async-start(bf16[256,8,128]{2,0,1:T(8,128)(2,1)} %copy.78), calls=%async_computation.2 | async-start | bytes 1048576 | tf_op jit(solution)/shard_map/all_to_all | solution.py:148
  163.1 231.8 %all-reduce.2.cloned.1.call-start = ((), (), s32[]{:S(2)}) async-start(), calls=%async_computation.6 | async-start | bytes 196608 | tf_op jit(solution)/shard_map/psum | solution.py:173
  182.6 4.6 collective-permute-start.1
  182.7 5.9 collective-permute-start.2
  182.8 8.2 %collective-permute-start.3 = (bf16[256,128]{0,1:T(8,128)(2,1)S(1)}, bf16[256,128]{0,1:T(8,128)(2,1)S(1)}, u32[]{:S(2)}, u32[]{:S(2)}) collective-permute-start(bf16[256,128]{0,1:T(8,128)(2,1)S(1)} %get-tuple-element.38), channel_id=1, source_target_pairs={{0,3},{1,2},{2,1},{3,0},{4,7},{5,6},{6,5},{7,4},{8,11},{9,10},{10,... | collective-permute-start | bytes 196616 | tf_op jit(solution)/shard_map/ppermute | solution.py:106
  184.6 11.0 %collective-permute-start.4 = (bf16[256,128]{0,1:T(8,128)(2,1)S(1)}, bf16[256,128]{0,1:T(8,128)(2,1)S(1)}, u32[]{:S(2)}, u32[]{:S(2)}) collective-permute-start(bf16[256,128]{0,1:T(8,128)(2,1)S(1)} %get-tuple-element.37), channel_id=1, source_target_pairs={{0,4},{1,5},{2,6},{3,7},{4,0},{5,1},{6,2},{7,3},{8,12},{9,13},{10,... | collective-permute-start | bytes 196616 | tf_op jit(solution)/shard_map/ppermute | solution.py:106
  184.7 11.7 %collective-permute-start.5 = (bf16[256,128]{0,1:T(8,128)(2,1)S(1)}, bf16[256,128]{0,1:T(8,128)(2,1)S(1)}, u32[]{:S(2)}, u32[]{:S(2)}) collective-permute-start(bf16[256,128]{0,1:T(8,128)(2,1)S(1)} %get-tuple-element.36), channel_id=1, source_target_pairs={{0,5},{1,4},{2,7},{3,6},{4,1},{5,0},{6,3},{7,2},{8,13},{9,12},{10,... | collective-permute-start | bytes 196616 | tf_op jit(solution)/shard_map/ppermute | solution.py:106
  187.3 9.2 %collective-permute-start.6 = (bf16[256,128]{0,1:T(8,128)(2,1)S(1)}, bf16[256,128]{0,1:T(8,128)(2,1)S(1)}, u32[]{:S(2)}, u32[]{:S(2)}) collective-permute-start(bf16[256,128]{0,1:T(8,128)(2,1)S(1)} %get-tuple-element.35), channel_id=1, source_target_pairs={{0,6},{1,7},{2,4},{3,5},{4,2},{5,3},{6,0},{7,1},{8,14},{9,15},{10,... | collective-permute-start | bytes 196616 | tf_op jit(solution)/shard_map/ppermute | solution.py:106
  188.6 7.9 %collective-permute-start.7 = (bf16[256,128]{0,1:T(8,128)(2,1)S(1)}, bf16[256,128]{0,1:T(8,128)(2,1)S(1)}, u32[]{:S(2)}, u32[]{:S(2)}) collective-permute-start(bf16[256,128]{0,1:T(8,128)(2,1)S(1)} %get-tuple-element.34), channel_id=1, source_target_pairs={{0,7},{1,6},{2,5},{3,4},{4,3},{5,2},{6,1},{7,0},{8,15},{9,14},{10,... | collective-permute-start | bytes 196616 | tf_op jit(solution)/shard_map/ppermute | solution.py:106
  217.9 6.1 copy-start.13
  217.9 6.1 copy-start.14
  231.8 4.3 copy-start.8
  238.9 4.8 copy-start.16
  245.4 20.1 %copy-start.11 = (f32[128,2048]{1,0:T(8,128)S(1)}, f32[128,2048]{1,0:T(8,128)}, u32[]{:S(2)}) copy-start(f32[128,2048]{1,0:T(8,128)} %copy-done.10) | copy-start | bytes 3145732
  266.8 3.1 collective-permute-start.8
  275.6 150.8 %reduce-scatter.3.cloned.1.call-start = ((), (), s32[]{:S(2)}) async-start(), calls=%async_computation.7 | async-start | bytes 1310720 | tf_op jit(solution)/shard_map/reduce_scatter | solution.py:153
  280.3 335.1 %reduce-scatter.5.cloned.1.call-start = ((), (), s32[]{:S(2)}) async-start(), calls=%async_computation.8 | async-start | bytes 17301504 | tf_op jit(solution)/shard_map/reduce_scatter | solution.py:129
  (10 other events, 21.1 us)
Sparse Core Ops, SparseCore 0:
  9.9 90.2 all-gather.1
  275.7 119.1 all-reduce.1
  397.8 28.5 reduce-scatter.2
  428.7 186.6 reduce-scatter.4
